TPU v7x, 256 devices: a whole 4x4x8 slice. The times are simulated.
256 devices in a mesh: ctx: 128 (over x, z, y_lo, core), head: 2 (over y_hi).
Axes of the slice: x: 4, y: 4 (y_hi: 2, y_lo: 2; y = y_hi * 2 + y_lo), z: 8, core: 2. Of those that a mesh axis runs over, the one named last changes fastest.
Arguments:
- queries: bfloat16 [32768, 512], P('ctx', 'head'), parts along dimension 1, may hold values from -32 to 32
- keys: bfloat16 [32768, 256], P('ctx', 'head'), parts along dimension 1, may hold values from -16 to 16
- values: bfloat16 [32768, 256], P('ctx', 'head'), parts along dimension 1, may hold values from -6 to 6
- doc_starts: int32 [6], P('head'), parts along dimension 0, may hold values from 1 to 12288, as said below
Outputs:
- attended: bfloat16 [32768, 512], P('ctx', 'head'), parts along dimension 1
There are 2 independent parts, one for each index of `head`. A program takes and returns all parts, laid end to end along the dimension named above; each array names one. Nothing has to cross between parts.
Inputs may be any that keep to these rules, and one draw needn't show every extreme that they name: `doc_starts`: strictly rising; the fourth document starts at exactly 12288.
All inputs are finite; a program needn't handle non-finite values.
Results may differ from a plain program's by a relative error of at most 0.01.
Values may be sent and summed in bfloat16 or wider, within the bound.
A program may use at most 64 MiB of HBM per device.

v0:
```python
import math
import jax
import jax.numpy as jnp
from jax import lax
from jax.sharding import PartitionSpec as P

D_HEAD = 128
Q_HEADS = 2
SCALE = 144.0 ** (-0.5)
NEGATIVE = -1e30


def doc_index(positions, doc_starts):
    return jnp.sum((positions[:, None] >= doc_starts[None, :]).astype(jnp.int32), axis=1)


def update_part(partial_value, target, key_block, block_start, doc_starts):
    query_rows, query_pos, query_doc, low_edge, high_edge = target
    key_count = key_block.shape[1]

    def attend(carried):
        row_max, row_total, weighted = carried
        key_pos = block_start + lax.iota(jnp.int32, key_count)
        key_doc = doc_index(key_pos, doc_starts)
        scores = (
            jnp.einsum("qhd,kd->hqk", query_rows, key_block[0], preferred_element_type=jnp.float32)
            * SCALE
        )
        visible = (key_pos[None, :] <= query_pos[:, None]) & (key_pos[None, :] >= low_edge)
        visible = (
            visible & (key_pos[None, :] < high_edge) & (key_doc[None, :] == query_doc[:, None])
        )
        scores = jnp.where(visible[None], scores, NEGATIVE)
        new_max = jnp.maximum(row_max, jnp.max(scores, axis=2))
        expo = jnp.where(visible[None], jnp.exp(scores - new_max[:, :, None]), 0.0)
        rescale = jnp.exp(row_max - new_max)
        row_total = row_total * rescale + jnp.sum(expo, axis=2)
        product = jnp.einsum(
            "hqk,kd->qhd",
            expo.astype(jnp.bfloat16),
            key_block[1],
            preferred_element_type=jnp.float32,
        )
        weighted = weighted * jnp.transpose(rescale)[:, :, None] + product
        return (new_max, row_total, weighted)

    needed = (block_start < high_edge) & (block_start + key_count > low_edge)
    return lax.cond(needed, attend, lambda carried: carried, partial_value)


def shards(queries, keys, values, doc_starts):
    shard_rows = queries.shape[0]
    my_index = lax.axis_index("ctx")
    row_iota = lax.iota(jnp.int32, shard_rows)
    own_pos = my_index * shard_rows + row_iota
    own_rows = queries.reshape(shard_rows, Q_HEADS, D_HEAD)
    own_doc = doc_index(own_pos, doc_starts)
    key_values = jnp.stack([keys, values])
    fresh_partial = (
        jnp.full((Q_HEADS, shard_rows), NEGATIVE, jnp.float32),
        jnp.zeros((Q_HEADS, shard_rows), jnp.float32),
        jnp.zeros((shard_rows, Q_HEADS, D_HEAD), jnp.float32),
    )
    targets = ((own_rows, own_pos, own_doc, jnp.int32(0), (my_index + 1) * shard_rows),)
    partials = tuple((fresh_partial for target in targets))
    shard_keys = lax.all_gather(key_values, "ctx", axis=1, tiled=True)
    key_total = shard_keys.shape[1]
    block_len = shard_rows * math.gcd(key_total // shard_rows, 4)

    def block_step(block_number, running):
        key_block = lax.dynamic_slice_in_dim(shard_keys, block_number * block_len, block_len, 1)
        block_start = block_number * block_len
        return tuple(
            (
                update_part(partial_value, target, key_block, block_start, doc_starts)
                for partial_value, target in zip(running, targets)
            )
        )

    partials = lax.fori_loop(0, key_total // block_len, block_step, partials)
    result = partials[0]
    row_max, row_total, weighted = result
    attended = weighted / jnp.transpose(row_total)[:, :, None]
    return attended.reshape(shard_rows, Q_HEADS * D_HEAD).astype(jnp.bfloat16)


def solution(mesh):
    in_specs = (P("ctx", "head"), P("ctx", "head"), P("ctx", "head"), P("head"))
    out_specs = P("ctx", "head")
    return jax.shard_map(shards, mesh=mesh, in_specs=in_specs, out_specs=out_specs, check_vma=False)
```

profile of v0, /device:TPU:230, one launch (start us, length us, event | category | flops | bytes accessed | tf_op | source)
XLA Modules:
  0.0 432.7 jit_solution(961604463259147152)
XLA Ops:
  10.0 225.3 %all-gather.2.cloned.1.call-done = bf16[2,32768,128]{2,1,0:T(8,128)(2,1)} async-done(((bf16[2,256,128]{2,1,0:T(8,128)(2,1)}), bf16[2,32768,128]{2,1,0:T(8,128)(2,1)}) %all-gather.2.cloned.1.call-update) | async-done | bytes 16777232 | tf_op jit(solution)/shard_map/all_gather | solution.py:66
  235.3 189.7 %while.18 = (s32[]{:T(128)}, f32[2,256]{1,0:T(2,128)S(1)}, f32[2,256]{1,0:T(2,128)S(1)}, f32[256,2,128]{2,0,1:T(8,128)S(1)}, s32[]{:T(128)}, /*index=5*/s32[3]{0...) while((s32[]{:T(128)}, f32[2,256]{1,0:T(2,128)S(1)}, ...), condition=%wide.region_7.8_spmd.clone, body=%wide.region_1.7_spmd.clone.sunk | while | flops 276707072 | bytes 8582549 | solution.py:80
  241.3 5.9 %conditional.3 = ((f32[2,256]{1,0:T(2,128)S(1)}, f32[2,256]{1,0:T(2,128)S(1)}, f32[256,2,128]{2,0,1:T(8,128)S(1)})) conditional(s32[]{:T(128)} %convert_element_type.37, (f32[2,256]{1,0:T(2,128)S(1)}, f32[2,256]{1,0:T(2,128)S(1)}, f32[256,2,128]{2,0,1:T(8,128)S(1)}) %tuple.50, (s32[]{:T(128)}, s32[]{:T(128)}, s32[]{:T(128)}, s32[3]{0:T(128)}, ...), branch_computations={%region_2.0_spmd, %region_3.6_spmd} | conditional | flops 276707072 | bytes 8581238 | solution.py:48
  247.2 5.9 %conditional.3 = ((f32[2,256]{1,0:T(2,128)S(1)}, f32[2,256]{1,0:T(2,128)S(1)}, f32[256,2,128]{2,0,1:T(8,128)S(1)})) conditional(s32[]{:T(128)} %convert_element_type.37, (f32[2,256]{1,0:T(2,128)S(1)}, f32[2,256]{1,0:T(2,128)S(1)}, f32[256,2,128]{2,0,1:T(8,128)S(1)}) %tuple.50, (s32[]{:T(128)}, s32[]{:T(128)}, s32[]{:T(128)}, s32[3]{0:T(128)}, ...), branch_computations={%region_2.0_spmd, %region_3.6_spmd} | conditional | flops 276707072 | bytes 8581238 | solution.py:48
  253.1 5.9 %conditional.3 = ((f32[2,256]{1,0:T(2,128)S(1)}, f32[2,256]{1,0:T(2,128)S(1)}, f32[256,2,128]{2,0,1:T(8,128)S(1)})) conditional(s32[]{:T(128)} %convert_element_type.37, (f32[2,256]{1,0:T(2,128)S(1)}, f32[2,256]{1,0:T(2,128)S(1)}, f32[256,2,128]{2,0,1:T(8,128)S(1)}) %tuple.50, (s32[]{:T(128)}, s32[]{:T(128)}, s32[]{:T(128)}, s32[3]{0:T(128)}, ...), branch_computations={%region_2.0_spmd, %region_3.6_spmd} | conditional | flops 276707072 | bytes 8581238 | solution.py:48
  259.1 5.9 %conditional.3 = ((f32[2,256]{1,0:T(2,128)S(1)}, f32[2,256]{1,0:T(2,128)S(1)}, f32[256,2,128]{2,0,1:T(8,128)S(1)})) conditional(s32[]{:T(128)} %convert_element_type.37, (f32[2,256]{1,0:T(2,128)S(1)}, f32[2,256]{1,0:T(2,128)S(1)}, f32[256,2,128]{2,0,1:T(8,128)S(1)}) %tuple.50, (s32[]{:T(128)}, s32[]{:T(128)}, s32[]{:T(128)}, s32[3]{0:T(128)}, ...), branch_computations={%region_2.0_spmd, %region_3.6_spmd} | conditional | flops 276707072 | bytes 8581238 | solution.py:48
  265.0 5.9 %conditional.3 = ((f32[2,256]{1,0:T(2,128)S(1)}, f32[2,256]{1,0:T(2,128)S(1)}, f32[256,2,128]{2,0,1:T(8,128)S(1)})) conditional(s32[]{:T(128)} %convert_element_type.37, (f32[2,256]{1,0:T(2,128)S(1)}, f32[2,256]{1,0:T(2,128)S(1)}, f32[256,2,128]{2,0,1:T(8,128)S(1)}) %tuple.50, (s32[]{:T(128)}, s32[]{:T(128)}, s32[]{:T(128)}, s32[3]{0:T(128)}, ...), branch_computations={%region_2.0_spmd, %region_3.6_spmd} | conditional | flops 276707072 | bytes 8581238 | solution.py:48
  270.9 5.9 %conditional.3 = ((f32[2,256]{1,0:T(2,128)S(1)}, f32[2,256]{1,0:T(2,128)S(1)}, f32[256,2,128]{2,0,1:T(8,128)S(1)})) conditional(s32[]{:T(128)} %convert_element_type.37, (f32[2,256]{1,0:T(2,128)S(1)}, f32[2,256]{1,0:T(2,128)S(1)}, f32[256,2,128]{2,0,1:T(8,128)S(1)}) %tuple.50, (s32[]{:T(128)}, s32[]{:T(128)}, s32[]{:T(128)}, s32[3]{0:T(128)}, ...), branch_computations={%region_2.0_spmd, %region_3.6_spmd} | conditional | flops 276707072 | bytes 8581238 | solution.py:48
  276.8 5.9 %conditional.3 = ((f32[2,256]{1,0:T(2,128)S(1)}, f32[2,256]{1,0:T(2,128)S(1)}, f32[256,2,128]{2,0,1:T(8,128)S(1)})) conditional(s32[]{:T(128)} %convert_element_type.37, (f32[2,256]{1,0:T(2,128)S(1)}, f32[2,256]{1,0:T(2,128)S(1)}, f32[256,2,128]{2,0,1:T(8,128)S(1)}) %tuple.50, (s32[]{:T(128)}, s32[]{:T(128)}, s32[]{:T(128)}, s32[3]{0:T(128)}, ...), branch_computations={%region_2.0_spmd, %region_3.6_spmd} | conditional | flops 276707072 | bytes 8581238 | solution.py:48
  282.8 5.9 %conditional.3 = ((f32[2,256]{1,0:T(2,128)S(1)}, f32[2,256]{1,0:T(2,128)S(1)}, f32[256,2,128]{2,0,1:T(8,128)S(1)})) conditional(s32[]{:T(128)} %convert_element_type.37, (f32[2,256]{1,0:T(2,128)S(1)}, f32[2,256]{1,0:T(2,128)S(1)}, f32[256,2,128]{2,0,1:T(8,128)S(1)}) %tuple.50, (s32[]{:T(128)}, s32[]{:T(128)}, s32[]{:T(128)}, s32[3]{0:T(128)}, ...), branch_computations={%region_2.0_spmd, %region_3.6_spmd} | conditional | flops 276707072 | bytes 8581238 | solution.py:48
  288.7 5.9 %conditional.3 = ((f32[2,256]{1,0:T(2,128)S(1)}, f32[2,256]{1,0:T(2,128)S(1)}, f32[256,2,128]{2,0,1:T(8,128)S(1)})) conditional(s32[]{:T(128)} %convert_element_type.37, (f32[2,256]{1,0:T(2,128)S(1)}, f32[2,256]{1,0:T(2,128)S(1)}, f32[256,2,128]{2,0,1:T(8,128)S(1)}) %tuple.50, (s32[]{:T(128)}, s32[]{:T(128)}, s32[]{:T(128)}, s32[3]{0:T(128)}, ...), branch_computations={%region_2.0_spmd, %region_3.6_spmd} | conditional | flops 276707072 | bytes 8581238 | solution.py:48
  294.6 5.9 %conditional.3 = ((f32[2,256]{1,0:T(2,128)S(1)}, f32[2,256]{1,0:T(2,128)S(1)}, f32[256,2,128]{2,0,1:T(8,128)S(1)})) conditional(s32[]{:T(128)} %convert_element_type.37, (f32[2,256]{1,0:T(2,128)S(1)}, f32[2,256]{1,0:T(2,128)S(1)}, f32[256,2,128]{2,0,1:T(8,128)S(1)}) %tuple.50, (s32[]{:T(128)}, s32[]{:T(128)}, s32[]{:T(128)}, s32[3]{0:T(128)}, ...), branch_computations={%region_2.0_spmd, %region_3.6_spmd} | conditional | flops 276707072 | bytes 8581238 | solution.py:48
  300.6 5.9 %conditional.3 = ((f32[2,256]{1,0:T(2,128)S(1)}, f32[2,256]{1,0:T(2,128)S(1)}, f32[256,2,128]{2,0,1:T(8,128)S(1)})) conditional(s32[]{:T(128)} %convert_element_type.37, (f32[2,256]{1,0:T(2,128)S(1)}, f32[2,256]{1,0:T(2,128)S(1)}, f32[256,2,128]{2,0,1:T(8,128)S(1)}) %tuple.50, (s32[]{:T(128)}, s32[]{:T(128)}, s32[]{:T(128)}, s32[3]{0:T(128)}, ...), branch_computations={%region_2.0_spmd, %region_3.6_spmd} | conditional | flops 276707072 | bytes 8581238 | solution.py:48
  306.5 5.9 %conditional.3 = ((f32[2,256]{1,0:T(2,128)S(1)}, f32[2,256]{1,0:T(2,128)S(1)}, f32[256,2,128]{2,0,1:T(8,128)S(1)})) conditional(s32[]{:T(128)} %convert_element_type.37, (f32[2,256]{1,0:T(2,128)S(1)}, f32[2,256]{1,0:T(2,128)S(1)}, f32[256,2,128]{2,0,1:T(8,128)S(1)}) %tuple.50, (s32[]{:T(128)}, s32[]{:T(128)}, s32[]{:T(128)}, s32[3]{0:T(128)}, ...), branch_computations={%region_2.0_spmd, %region_3.6_spmd} | conditional | flops 276707072 | bytes 8581238 | solution.py:48
  312.4 5.9 %conditional.3 = ((f32[2,256]{1,0:T(2,128)S(1)}, f32[2,256]{1,0:T(2,128)S(1)}, f32[256,2,128]{2,0,1:T(8,128)S(1)})) conditional(s32[]{:T(128)} %convert_element_type.37, (f32[2,256]{1,0:T(2,128)S(1)}, f32[2,256]{1,0:T(2,128)S(1)}, f32[256,2,128]{2,0,1:T(8,128)S(1)}) %tuple.50, (s32[]{:T(128)}, s32[]{:T(128)}, s32[]{:T(128)}, s32[3]{0:T(128)}, ...), branch_computations={%region_2.0_spmd, %region_3.6_spmd} | conditional | flops 276707072 | bytes 8581238 | solution.py:48
  318.3 5.9 %conditional.3 = ((f32[2,256]{1,0:T(2,128)S(1)}, f32[2,256]{1,0:T(2,128)S(1)}, f32[256,2,128]{2,0,1:T(8,128)S(1)})) conditional(s32[]{:T(128)} %convert_element_type.37, (f32[2,256]{1,0:T(2,128)S(1)}, f32[2,256]{1,0:T(2,128)S(1)}, f32[256,2,128]{2,0,1:T(8,128)S(1)}) %tuple.50, (s32[]{:T(128)}, s32[]{:T(128)}, s32[]{:T(128)}, s32[3]{0:T(128)}, ...), branch_computations={%region_2.0_spmd, %region_3.6_spmd} | conditional | flops 276707072 | bytes 8581238 | solution.py:48
  324.3 5.9 %conditional.3 = ((f32[2,256]{1,0:T(2,128)S(1)}, f32[2,256]{1,0:T(2,128)S(1)}, f32[256,2,128]{2,0,1:T(8,128)S(1)})) conditional(s32[]{:T(128)} %convert_element_type.37, (f32[2,256]{1,0:T(2,128)S(1)}, f32[2,256]{1,0:T(2,128)S(1)}, f32[256,2,128]{2,0,1:T(8,128)S(1)}) %tuple.50, (s32[]{:T(128)}, s32[]{:T(128)}, s32[]{:T(128)}, s32[3]{0:T(128)}, ...), branch_computations={%region_2.0_spmd, %region_3.6_spmd} | conditional | flops 276707072 | bytes 8581238 | solution.py:48
  330.2 5.9 %conditional.3 = ((f32[2,256]{1,0:T(2,128)S(1)}, f32[2,256]{1,0:T(2,128)S(1)}, f32[256,2,128]{2,0,1:T(8,128)S(1)})) conditional(s32[]{:T(128)} %convert_element_type.37, (f32[2,256]{1,0:T(2,128)S(1)}, f32[2,256]{1,0:T(2,128)S(1)}, f32[256,2,128]{2,0,1:T(8,128)S(1)}) %tuple.50, (s32[]{:T(128)}, s32[]{:T(128)}, s32[]{:T(128)}, s32[3]{0:T(128)}, ...), branch_computations={%region_2.0_spmd, %region_3.6_spmd} | conditional | flops 276707072 | bytes 8581238 | solution.py:48
  336.1 5.9 %conditional.3 = ((f32[2,256]{1,0:T(2,128)S(1)}, f32[2,256]{1,0:T(2,128)S(1)}, f32[256,2,128]{2,0,1:T(8,128)S(1)})) conditional(s32[]{:T(128)} %convert_element_type.37, (f32[2,256]{1,0:T(2,128)S(1)}, f32[2,256]{1,0:T(2,128)S(1)}, f32[256,2,128]{2,0,1:T(8,128)S(1)}) %tuple.50, (s32[]{:T(128)}, s32[]{:T(128)}, s32[]{:T(128)}, s32[3]{0:T(128)}, ...), branch_computations={%region_2.0_spmd, %region_3.6_spmd} | conditional | flops 276707072 | bytes 8581238 | solution.py:48
  342.1 5.9 %conditional.3 = ((f32[2,256]{1,0:T(2,128)S(1)}, f32[2,256]{1,0:T(2,128)S(1)}, f32[256,2,128]{2,0,1:T(8,128)S(1)})) conditional(s32[]{:T(128)} %convert_element_type.37, (f32[2,256]{1,0:T(2,128)S(1)}, f32[2,256]{1,0:T(2,128)S(1)}, f32[256,2,128]{2,0,1:T(8,128)S(1)}) %tuple.50, (s32[]{:T(128)}, s32[]{:T(128)}, s32[]{:T(128)}, s32[3]{0:T(128)}, ...), branch_computations={%region_2.0_spmd, %region_3.6_spmd} | conditional | flops 276707072 | bytes 8581238 | solution.py:48
  348.0 5.9 %conditional.3 = ((f32[2,256]{1,0:T(2,128)S(1)}, f32[2,256]{1,0:T(2,128)S(1)}, f32[256,2,128]{2,0,1:T(8,128)S(1)})) conditional(s32[]{:T(128)} %convert_element_type.37, (f32[2,256]{1,0:T(2,128)S(1)}, f32[2,256]{1,0:T(2,128)S(1)}, f32[256,2,128]{2,0,1:T(8,128)S(1)}) %tuple.50, (s32[]{:T(128)}, s32[]{:T(128)}, s32[]{:T(128)}, s32[3]{0:T(128)}, ...), branch_computations={%region_2.0_spmd, %region_3.6_spmd} | conditional | flops 276707072 | bytes 8581238 | solution.py:48
  353.9 5.9 %conditional.3 = ((f32[2,256]{1,0:T(2,128)S(1)}, f32[2,256]{1,0:T(2,128)S(1)}, f32[256,2,128]{2,0,1:T(8,128)S(1)})) conditional(s32[]{:T(128)} %convert_element_type.37, (f32[2,256]{1,0:T(2,128)S(1)}, f32[2,256]{1,0:T(2,128)S(1)}, f32[256,2,128]{2,0,1:T(8,128)S(1)}) %tuple.50, (s32[]{:T(128)}, s32[]{:T(128)}, s32[]{:T(128)}, s32[3]{0:T(128)}, ...), branch_computations={%region_2.0_spmd, %region_3.6_spmd} | conditional | flops 276707072 | bytes 8581238 | solution.py:48
  359.8 5.9 %conditional.3 = ((f32[2,256]{1,0:T(2,128)S(1)}, f32[2,256]{1,0:T(2,128)S(1)}, f32[256,2,128]{2,0,1:T(8,128)S(1)})) conditional(s32[]{:T(128)} %convert_element_type.37, (f32[2,256]{1,0:T(2,128)S(1)}, f32[2,256]{1,0:T(2,128)S(1)}, f32[256,2,128]{2,0,1:T(8,128)S(1)}) %tuple.50, (s32[]{:T(128)}, s32[]{:T(128)}, s32[]{:T(128)}, s32[3]{0:T(128)}, ...), branch_computations={%region_2.0_spmd, %region_3.6_spmd} | conditional | flops 276707072 | bytes 8581238 | solution.py:48
  419.1 5.9 %conditional.3 = ((f32[2,256]{1,0:T(2,128)S(1)}, f32[2,256]{1,0:T(2,128)S(1)}, f32[256,2,128]{2,0,1:T(8,128)S(1)})) conditional(s32[]{:T(128)} %convert_element_type.37, (f32[2,256]{1,0:T(2,128)S(1)}, f32[2,256]{1,0:T(2,128)S(1)}, f32[256,2,128]{2,0,1:T(8,128)S(1)}) %tuple.50, (s32[]{:T(128)}, s32[]{:T(128)}, s32[]{:T(128)}, s32[3]{0:T(128)}, ...), branch_computations={%region_2.0_spmd, %region_3.6_spmd} | conditional | flops 276707072 | bytes 8581238 | solution.py:48
  (405 shorter events, 248.7 us)
Async XLA Ops:
  6.5 228.7 %all-gather.2.cloned.1.call-start = ((), (), s32[]{:S(2)}) async-start(), calls=%async_computation | async-start | bytes 16908288 | tf_op jit(solution)/shard_map/all_gather | solution.py:66
Sparse Core Ops, SparseCore 0:
  9.2 226.0 all-gather.1
where the time goes:
time: 435 us; the launch traced here: 433 us
  waiting for transfers between devices  225 us (52%)
  matrix products  104 us (24%)
  other arithmetic  84.4 us (19%)
  between operations  13.4 us (3%)
    all_gather x1, waiting for transfers between devices, shards(): shard_keys = lax.all_gather(key_values, 'ctx', axis=1, tiled=True)  225 us
    dot_general x32, matrix products, attend(): jnp.einsum('hqk,kd->qhd', expo.astype(jnp.bfloat16), key_block[1], prefer...  59 us
    dot_general x32, matrix products, attend(): jnp.einsum('qhd,kd->hqk', query_rows, key_block[0], preferred_element_typ...  45.2 us
    and x32, other arithmetic, attend(): visible & (key_pos[None, :] < high_edge)  38.2 us
    reduce_sum x33, other arithmetic, doc_index(): jnp.sum((positions[:, None] >= doc_starts[None, :]).astype(jnp.int32), ax...  24.4 us
    reduce_sum x32, other arithmetic, attend(): row_total = row_total * rescale + jnp.sum(expo, axis=2)  18.1 us
  transfers between devices with their start and end apart: 1, of which 1 were waited for; matrix products, arithmetic and copies ran while one was open for 0% of the time, Pallas kernels for 0%

commit v1 on v0

--- a/solution.py
+++ b/solution.py
@@ -63,7 +63,9 @@
     )
     targets = ((own_rows, own_pos, own_doc, jnp.int32(0), (my_index + 1) * shard_rows),)
     partials = tuple((fresh_partial for target in targets))
-    shard_keys = lax.all_gather(key_values, "ctx", axis=1, tiled=True)
+    shard_keys = jnp.concatenate(
+        lax.all_to_all(jnp.stack([key_values] * lax.axis_size("ctx")), "ctx", 0, 0), axis=1
+    )
     key_total = shard_keys.shape[1]
     block_len = shard_rows * math.gcd(key_total // shard_rows, 4)
 

time: 435 us -> 567 us (1.30)
  waiting for transfers between devices: 225 us -> 363 us
  other arithmetic: 84.4 us -> 62 us
  local copies, waits for them, and re-layouts: 1.31 us -> 20.8 us
  between operations: 13.4 us -> 0.08 us
  starting transfers between devices: 0.01 us -> 11.9 us
    all_to_all x0 -> x1, waiting for transfers between devices: none -> 363 us  [shards(): lax.all_to_all(jnp.stack([key_values] * lax.axis_size('ctx')), 'ctx', 0, 0)]
    all_gather x1 -> x0, waiting for transfers between devices: 225 us -> none  [shards(): shard_keys = lax.all_gather(key_values, 'ctx', axis=1, tiled=True)]
    reduce_sum x33, other arithmetic: 24.4 us -> 2.73 us  [doc_index(): jnp.sum((positions[:, None] >= doc_starts[None, :]).astype(jnp.int32), ax...]
    all_to_all x0 -> x1, local copies, waits for them, and re-layouts: none -> 14.1 us  [shards(): lax.all_to_all(jnp.stack([key_values] * lax.axis_size('ctx')), 'ctx', 0, 0)]
    all_to_all x0 -> x1, starting transfers between devices: none -> 11.9 us  [shards(): lax.all_to_all(jnp.stack([key_values] * lax.axis_size('ctx')), 'ctx', 0, 0)]
    another operation x0 -> x1, local copies, waits for them, and re-layouts: none -> 6.32 us  [shards(): jnp.stack([key_values] * lax.axis_size('ctx'))]
where the time goes in v1:
time: 567 us; the launch traced here: 565 us
  waiting for transfers between devices  363 us (64%)
  matrix products  103 us (18%)
  other arithmetic  62 us (11%)
  local copies, waits for them, and re-layouts  20.8 us (4%)
  starting transfers between devices  11.9 us (2%)
    all_to_all x1, waiting for transfers between devices, shards(): lax.all_to_all(jnp.stack([key_values] * lax.axis_size('ctx')), 'ctx', 0, 0)  363 us
    dot_general x32, matrix products, attend(): jnp.einsum('hqk,kd->qhd', expo.astype(jnp.bfloat16), key_block[1], prefer...  58.4 us
    dot_general x32, matrix products, attend(): jnp.einsum('qhd,kd->hqk', query_rows, key_block[0], preferred_element_typ...  45 us
    and x32, other arithmetic, attend(): visible & (key_pos[None, :] < high_edge)  38.2 us
    reduce_sum x32, other arithmetic, attend(): row_total = row_total * rescale + jnp.sum(expo, axis=2)  18.1 us
    all_to_all x1, local copies, waits for them, and re-layouts, shards(): lax.all_to_all(jnp.stack([key_values] * lax.axis_size('ctx')), 'ctx', 0, 0)  14.1 us
    all_to_all x1, starting transfers between devices, shards(): lax.all_to_all(jnp.stack([key_values] * lax.axis_size('ctx')), 'ctx', 0, 0)  11.9 us
  transfers between devices with their start and end apart: 1, of which 1 were waited for; matrix products, arithmetic and copies ran while one was open for 0% of the time, Pallas kernels for 0%

profile of v1, /device:TPU:230, one launch (start us, length us, event | category | flops | bytes accessed | tf_op | source)
XLA Modules:
  0.0 564.6 jit_solution(10574905336456455535)
XLA Ops:
  0.9 6.3 %stack.11 = bf16[128,2,256,128]{3,2,1,0:T(8,128)(2,1)} broadcast(bf16[2,256,128]{2,1,0:T(8,128)(2,1)S(1)} %pad_maximum_fusion), dimensions={1,2,3} | broadcast | bytes 16908288 | tf_op jit(solution)/shard_map/stack | solution.py:67
  7.2 11.9 %all-to-all-start = ((bf16[128,2,256,128]{3,2,1,0:T(8,128)(2,1)}), bf16[128,2,256,128]{3,2,1,0:T(8,128)(2,1)}, u32[]{:S(2)}, u32[]{:S(2)}) async-start(bf16[128,2,256,128]{3,2,1,0:T(8,128)(2,1)} %stack.11), calls=%async_computation | async-start | bytes 33554432 | tf_op jit(solution)/shard_map/all_to_all | solution.py:67
  19.5 362.5 %all-to-all-done = bf16[128,2,256,128]{3,2,1,0:T(8,128)(2,1)} async-done(((bf16[128,2,256,128]{3,2,1,0:T(8,128)(2,1)}), bf16[128,2,256,128]{3,2,1,0:T(8,128)(2,1)}, u32[]{:S(2)}, u32[]{:S(2)}) %all-to-all-start) | async-done | bytes 16777248 | tf_op jit(solution)/shard_map/all_to_all | solution.py:67
  382.0 14.1 %copy.21 = bf16[128,2,256,128]{3,2,0,1:T(8,128)(2,1)} copy(bf16[128,2,256,128]{3,2,1,0:T(8,128)(2,1)} %all-to-all-done) | data formatting | bytes 33554432 | tf_op jit(solution)/shard_map/all_to_all | solution.py:67
  396.1 167.8 %while.18 = (s32[]{:T(128)}, f32[2,256]{1,0:T(2,128)S(1)}, f32[2,256]{1,0:T(2,128)S(1)}, f32[256,2,128]{2,0,1:T(8,128)S(1)}, s32[]{:T(128)}, /*index=5*/s32[3]{0...) while((s32[]{:T(128)}, f32[2,256]{1,0:T(2,128)S(1)}, ...), condition=%wide.region_7.8_spmd.clone, body=%wide.region_1.7_spmd.clone.sunk | while | flops 276707072 | bytes 8582549 | solution.py:82
  396.1 5.2 conditional.3
  401.4 5.2 conditional.3
  406.6 5.2 conditional.3
  417.1 5.2 conditional.3
  422.3 5.2 conditional.3
  427.6 5.2 conditional.3
  438.1 5.2 conditional.3
  443.3 5.2 conditional.3
  448.5 5.2 conditional.3
  459.0 5.2 conditional.3
  469.5 5.2 conditional.3
  480.0 5.2 conditional.3
  490.5 5.2 conditional.3
  501.0 5.2 conditional.3
  511.5 5.2 conditional.3
  521.9 5.2 conditional.3
  532.4 5.2 conditional.3
  542.9 5.2 conditional.3
  553.4 5.2 conditional.3
  (410 shorter events, 233.4 us)
Async XLA Ops:
  7.2 11.9 %copy-start = (bf16[256,256]{1,0:T(8,128)(2,1)S(1)}, bf16[256,256]{1,0:T(8,128)(2,1)}, u32[]{:S(2)}) copy-start(bf16[256,256]{1,0:T(8,128)(2,1)} %param.8) | copy-start | bytes 393220
  7.2 12.2 %copy-start.1 = (s32[3]{0:T(128)S(1)}, s32[3]{0:T(128)}, u32[]{:S(2)}) copy-start(s32[3]{0:T(128)} %param.11) | copy-start | bytes 40
  7.2 374.8 %all-to-all-start = ((bf16[128,2,256,128]{3,2,1,0:T(8,128)(2,1)}), bf16[128,2,256,128]{3,2,1,0:T(8,128)(2,1)}, u32[]{:S(2)}, u32[]{:S(2)}) async-start(bf16[128,2,256,128]{3,2,1,0:T(8,128)(2,1)} %stack.11), calls=%async_computation | async-start | bytes 33554432 | tf_op jit(solution)/shard_map/all_to_all | solution.py:67
